TPU v7x, 32 devices: a whole 2x2x4 slice. The times are simulated.
32 devices in a mesh: depth: 2 (over core), row: 4 (over y, x), col: 4 (over z).
Axes of the slice: x: 2, y: 2, z: 4, core: 2. Of those that a mesh axis runs over, the one named last changes fastest.
Arguments:
- tile_left: bfloat16 [16, 16, 64, 1024], P('row', 'col'), may hold values from -6 to 6
- tile_right: bfloat16 [16, 16, 64, 1024], P('row', 'col'), may hold values from -6 to 6
- row_left: bfloat16 [16, 8, 64, 1024], P('row', 'depth', None, 'col'), may hold values from -6 to 6
- row_right: bfloat16 [16, 8, 64, 1024], P('row', 'depth', None, 'col'), may hold values from -0.1875 to 0.1875
- col_left: bfloat16 [16, 8, 64, 1024], P('col', 'depth', None, 'row'), may hold values from -6 to 6
- col_right: bfloat16 [16, 8, 64, 1024], P('col', 'depth', None, 'row'), may hold values from -0.1875 to 0.1875
- row_mask: int32 [16, 8], P('row', 'depth'), may hold values 0 or 1
- col_mask: int32 [16, 8], P('col', 'depth'), may hold values 0 or 1
- sketch: bfloat16 [64, 1024], replicated, may hold values from -1 to 1
Outputs:
- new_left: float32 [16, 16, 64, 1024], P('row', 'col', 'depth')
- new_right: float32 [16, 16, 64, 1024], P('row', 'col', 'depth')
All inputs are finite; a program needn't handle non-finite values. No bound on the sum of `row_mask` or of `col_mask` on one device may be relied on, other than what follows from the above.
Results may differ from a plain program's by a relative error of at most 0.0003.
Values may be sent and summed in bfloat16 or wider, within the bound.
No kernel may reach another device: no remote copies, remote signals or barrier semaphores. Data moves between devices by JAX's collectives and lax.ppermute only.
A program may use at most 64 MiB of HBM per device.

v0:
```python
import math
import jax
import jax.numpy as jnp
from jax import lax
from jax.sharding import PartitionSpec as P

NB = 1024
K = 64
exact_mode = lax.Precision.HIGHEST


def orthonormalize(sketched):
    for repeat in range(2):
        gram_mat = jnp.einsum("ijtn,ijsn->ijts", sketched, sketched, precision=exact_mode)
        factor = jnp.linalg.cholesky(gram_mat)
        sketched = jax.scipy.linalg.solve_triangular(factor, sketched, lower=True)
    return sketched


def on_device(
    tile_left, tile_right, row_left, row_right, col_left, col_right, row_mask, col_mask, sketch
):
    row_full_left, row_full_right = (
        lax.all_gather(row_left, "col", axis=3, tiled=True),
        lax.all_gather(row_right, "col", axis=3, tiled=True),
    )
    col_full_left, col_full_right = (
        lax.all_gather(col_left, "row", axis=3, tiled=True),
        lax.all_gather(col_right, "row", axis=3, tiled=True),
    )
    weight_table = (
        row_mask.astype(jnp.float32)[:, None, :] * col_mask.astype(jnp.float32)[None, :, :]
    )
    coupling = jnp.einsum(
        "ikrn,jksn->ijkrs", row_full_right, col_full_right, preferred_element_type=jnp.float32
    )
    coupling = coupling * weight_table[:, :, :, None, None]
    col_sketch = jnp.einsum(
        "jksn,tn->jkst", col_full_left, sketch, preferred_element_type=jnp.float32
    )
    mixing = jnp.einsum("ijkrs,jkst->ijkrt", coupling, col_sketch, precision=exact_mode)
    partial_sketch = -jnp.einsum(
        "ijkrt,ikrn->ijtn",
        mixing,
        row_full_left,
        precision=exact_mode,
        preferred_element_type=jnp.float32,
    )
    sketch_right = jnp.einsum(
        "ijrn,tn->ijrt", tile_right, sketch, preferred_element_type=jnp.float32
    )
    summed = lax.psum(partial_sketch, "depth")
    sketched = summed + jnp.einsum(
        "ijrt,ijrn->ijtn",
        sketch_right,
        tile_left,
        precision=exact_mode,
        preferred_element_type=jnp.float32,
    )
    basis = orthonormalize(sketched)
    rank_rows = K // lax.axis_size("depth")
    rank_offset = lax.axis_index("depth") * rank_rows
    basis_mine = lax.dynamic_slice_in_dim(basis, rank_offset, rank_rows, 2)
    basis_row = jnp.einsum(
        "ijtn,ikrn->ijktr",
        basis,
        row_full_left,
        precision=exact_mode,
        preferred_element_type=jnp.float32,
    )
    projected = jnp.einsum("ijktr,ijkrs->ijkts", basis_row, coupling, precision=exact_mode)
    right_part = -jnp.einsum(
        "ijkts,jksn->ijtn",
        projected,
        col_full_left,
        precision=exact_mode,
        preferred_element_type=jnp.float32,
    )
    right_share = lax.psum_scatter(right_part, "depth", scatter_dimension=2, tiled=True)
    own_part = jnp.einsum(
        "ijtn,ijrn->ijtr",
        basis_mine,
        tile_left,
        precision=exact_mode,
        preferred_element_type=jnp.float32,
    )
    right_share = right_share + jnp.einsum(
        "ijtr,ijrn->ijtn",
        own_part,
        tile_right,
        precision=exact_mode,
        preferred_element_type=jnp.float32,
    )
    return (basis_mine * math.sqrt(NB), right_share / math.sqrt(NB))


def solution(mesh):
    in_specs = (
        P("row", "col", None, None),
        P("row", "col", None, None),
        P("row", "depth", None, "col"),
        P("row", "depth", None, "col"),
        P("col", "depth", None, "row"),
        P("col", "depth", None, "row"),
        P("row", "depth"),
        P("col", "depth"),
        P(),
    )
    out_specs = (P("row", "col", "depth", None), P("row", "col", "depth", None))
    return jax.shard_map(
        on_device, mesh=mesh, in_specs=in_specs, out_specs=out_specs, check_vma=False
    )
```

profile of v0, /device:TPU:0, one launch (start us, length us, event | category | flops | bytes accessed | tf_op | source)
XLA Modules:
  0.0 626.7 jit_solution(12347719536717495241)
XLA Ops:
  7.3 0.7 all-gather.5.cloned.1.call-update
  8.0 1.9 copy.21
  10.0 0.8 copy.22
  10.9 0.5 all-gather.11.cloned.1.call-update
  11.5 0.1 copy.23
  11.6 0.1 copy.24
  11.8 35.9 %all-gather.5.cloned.1.call-done = bf16[4,4,64,1024]{3,2,1,0:T(8,128)(2,1)} async-done(((bf16[4,4,64,256]{3,2,1,0:T(8,128)(2,1)}), bf16[4,4,64,1024]{3,2,1,0:T(8,128)(2,1)}) %all-gather.5.cloned.1.call-update) | async-done | bytes 2097168 | tf_op jit(solution)/shard_map/all_gather | solution.py:28
  47.7 2.3 convolution_bitcast_fusion
  49.9 35.2 %all-gather.7.cloned.1.call-done = bf16[4,4,64,1024]{3,2,0,1:T(8,128)(2,1)} async-done(((bf16[4,4,64,256]{3,2,0,1:T(8,128)(2,1)}), bf16[4,4,64,1024]{3,2,0,1:T(8,128)(2,1)}) %all-gather.7.cloned.1.call-update) | async-done | bytes 2097168 | tf_op jit(solution)/shard_map/all_gather | solution.py:29
  85.1 48.4 %all-gather.9.cloned.1.call-done = bf16[4,4,64,1024]{3,2,0,1:T(8,128)(2,1)} async-done(((bf16[4,4,64,256]{3,2,0,1:T(8,128)(2,1)}), bf16[4,4,64,1024]{3,2,0,1:T(8,128)(2,1)}) %all-gather.9.cloned.1.call-update) | async-done | bytes 2097168 | tf_op jit(solution)/shard_map/all_gather | solution.py:25
  133.6 3.5 bitcast_multiply_fusion
  137.1 1.3 copy-done.6
  138.4 3.3 fusion.15
  141.7 37.8 %all-gather.11.cloned.1.call-done = bf16[4,4,64,1024]{3,2,1,0:T(8,128)(2,1)} async-done(((bf16[4,4,64,256]{3,2,1,0:T(8,128)(2,1)}), bf16[4,4,64,1024]{3,2,1,0:T(8,128)(2,1)}) %all-gather.11.cloned.1.call-update) | async-done | bytes 2097168 | tf_op jit(solution)/shard_map/all_gather | solution.py:24
  179.5 6.2 bitcast_negate_fusion.1
  185.6 0.3 reduce-scatter.2.cloned.1.call-start
  186.0 2.7 fusion.32
  188.7 23.4 %all-reduce.2.cloned.1.call-done = f32[4,4,64,1024]{3,2,1,0:T(8,128)} async-done(((f32[4,4,64,1024]{3,2,1,0:T(8,128)}), f32[4,4,64,1024]{3,2,1,0:T(8,128)}) %all-reduce.2.cloned.1.call-update) | async-done | bytes 4194320 | tf_op jit(solution)/shard_map/psum | solution.py:52
  212.1 4.1 convolution_add_fusion
  216.2 1.9 copy-done.2
  218.2 4.0 fusion.36
  222.2 0.2 copy.25
  222.4 0.9 fusion.30
  223.3 95.0 %custom-call.8 = f32[4,4,64,64]{3,2,1,0:T(8,128)S(1)} custom-call(f32[4,4,64,64]{3,2,1,0:T(8,128)} %fusion.30), custom_call_target="Cholesky" | custom-call | tf_op jit(solution)/shard_map/jit(cholesky)/cholesky | solution.py:15
  318.3 0.1 select_reduce_fusion.1
  318.3 0.1 compare_reduce_fusion.1
  318.5 0.1 select_bitcast_fusion.1
  318.6 78.6 %custom-call.9 = f32[4,4,1,64,64]{3,4,2,1,0:T(8,128)S(1)} custom-call(f32[4,4,1,64,64]{4,3,2,1,0:T(8,128)S(1)} %select_bitcast_fusion.1), custom_call_target="InvertDiagBlocksLowerTriangular" | custom-call | tf_op jit(solution)/shard_map/jit(_solve_triangular)/vmap(vmap())/triangular_solve | solution.py:16
  397.3 5.5 fusion.28
  402.8 1.9 copy-done.1
  404.7 4.0 fusion.37
  408.8 0.2 copy.27
  409.0 0.9 fusion.27
  409.8 94.5 %custom-call.10 = f32[4,4,64,64]{3,2,1,0:T(8,128)S(1)} custom-call(f32[4,4,64,64]{3,2,1,0:T(8,128)} %fusion.27), custom_call_target="Cholesky" | custom-call | tf_op jit(solution)/shard_map/jit(cholesky)/cholesky | solution.py:15
  504.4 0.1 compare_reduce_fusion
  504.6 0.1 select_bitcast_fusion
  504.7 78.6 %custom-call.11 = f32[4,4,1,64,64]{3,4,2,1,0:T(8,128)S(1)} custom-call(f32[4,4,1,64,64]{4,3,2,1,0:T(8,128)S(1)} %select_bitcast_fusion), custom_call_target="InvertDiagBlocksLowerTriangular" | custom-call | tf_op jit(solution)/shard_map/jit(_solve_triangular)/vmap(vmap())/triangular_solve | solution.py:16
  583.4 5.8 fusion.25
  589.2 3.5 fusion
  592.7 1.4 copy.61
  594.1 0.2 copy-done.7
  594.2 3.5 fusion.12
  597.8 3.7 fusion.2
  601.5 3.4 dynamic-slice_multiply_fusion
  604.9 1.8 fusion.17
  606.7 8.1 %reduce-scatter.2.cloned.1.call-done = f32[4,4,32,1024]{3,2,0,1:T(8,128)} async-done(((f32[4,4,64,1024]{3,2,0,1:T(8,128)}), f32[4,4,32,1024]{3,2,0,1:T(8,128)}) %reduce-scatter.2.cloned.1.call-update) | async-done | bytes 2097168 | tf_op jit(solution)/shard_map/reduce_scatter | solution.py:79
  614.8 3.3 add_multiply_fusion
  618.2 1.5 copy.30
  (37 shorter events, 0.5 us)
Async XLA Ops:
  7.2 204.9 %copy-start = (bf16[4,4,64,1024]{3,2,1,0:T(8,128)(2,1)S(1)}, bf16[4,4,64,1024]{3,2,1,0:T(8,128)(2,1)}, u32[]{:S(2)}) copy-start(bf16[4,4,64,1024]{3,2,1,0:T(8,128)(2,1)} %param.12) | copy-start | bytes 6291460
  7.2 2.8 copy-start.9
  7.2 4.3 copy-start.11
  7.2 4.4 copy-start.12
  7.2 40.4 %copy-start.10 = (bf16[64,1024]{1,0:T(8,128)(2,1)S(1)}, bf16[64,1024]{1,0:T(8,128)(2,1)}, u32[]{:S(2)}) copy-start(bf16[64,1024]{1,0:T(8,128)(2,1)} %param.20) | copy-start | bytes 393220
  7.2 40.4 %all-gather.5.cloned.1.call-start = ((), (), s32[]{:S(2)}) async-start(), calls=%async_computation.1 | async-start | bytes 2621440 | tf_op jit(solution)/shard_map/all_gather | solution.py:28
  8.0 77.2 %all-gather.7.cloned.1.call-start = ((), (), s32[]{:S(2)}) async-start(), calls=%async_computation.2 | async-start | bytes 2621440 | tf_op jit(solution)/shard_map/all_gather | solution.py:29
  9.9 123.6 %all-gather.9.cloned.1.call-start = ((), (), s32[]{:S(2)}) async-start(), calls=%async_computation.3 | async-start | bytes 2621440 | tf_op jit(solution)/shard_map/all_gather | solution.py:25
  10.8 168.6 %all-gather.11.cloned.1.call-start = ((), (), s32[]{:S(2)}) async-start(), calls=%async_computation.4 | async-start | bytes 2621440 | tf_op jit(solution)/shard_map/all_gather | solution.py:24
  11.4 200.7 %all-reduce.2.cloned.1.call-start = ((), (), s32[]{:S(2)}) async-start(), calls=%async_computation.5 | async-start | bytes 8388608 | tf_op jit(solution)/shard_map/psum | solution.py:52
  137.1 1.3 copy-start.6
  185.6 429.2 %reduce-scatter.2.cloned.1.call-start = ((), (), s32[]{:S(2)}) async-start(), calls=%async_computation.6 | async-start | bytes 6291456 | tf_op jit(solution)/shard_map/reduce_scatter | solution.py:79
  216.2 1.9 copy-start.2
  402.8 1.9 copy-start.1
  583.3 5.8 copy-start.5
  589.2 3.5 copy-start.3
  592.6 1.6 copy-start.7
  594.2 3.5 copy-start.8
  601.5 3.4 copy-start.4
Sparse Core Ops, SparseCore 0:
  9.9 37.7 all-gather.4
  50.1 35.0 all-gather.6
  87.3 46.2 all-gather.8
  135.0 44.4 all-gather.10
  185.8 26.2 all-reduce.1
  601.6 13.2 reduce-scatter.1
where the time goes:
time: 632 us; the launch traced here: 627 us
  other arithmetic  353 us (56%)
  waiting for transfers between devices  190 us (30%)
  matrix products  57.2 us (9%)
  between operations  14.6 us (2%)
  local copies, waits for them, and re-layouts  11.6 us (2%)
    another operation x7, other arithmetic, orthonormalize(): factor = jnp.linalg.cholesky(gram_mat)  190 us
    another operation x5, other arithmetic, orthonormalize(): sketched = jax.scipy.linalg.solve_triangular(factor, sketched, lower=True)  158 us
    all_gather x1, waiting for transfers between devices, on_device(): lax.all_gather(row_right, 'col', axis=3, tiled=True)  48.4 us
    all_gather x1, waiting for transfers between devices, on_device(): lax.all_gather(row_left, 'col', axis=3, tiled=True)  37.8 us
    all_gather x1, waiting for transfers between devices, on_device(): lax.all_gather(col_left, 'row', axis=3, tiled=True)  35.9 us
    all_gather x1, waiting for transfers between devices, on_device(): lax.all_gather(col_right, 'row', axis=3, tiled=True)  35.2 us
    psum x1, waiting for transfers between devices, on_device(): summed = lax.psum(partial_sketch, 'depth')  23.4 us
  transfers between devices with their start and end apart: 6, of which 6 were waited for; matrix products, arithmetic and copies ran while one was open for 3% of the time, Pallas kernels for 0%

commit v1 on v0

--- a/solution.py
+++ b/solution.py
@@ -7,6 +7,19 @@
 NB = 1024
 K = 64
 exact_mode = lax.Precision.HIGHEST
+
+
+def ring_gather(x, axis, dim):
+    ways = lax.axis_size(axis)
+    up = [(d, (d + 1) % ways) for d in range(ways)]
+    down = [(d, (d - 1) % ways) for d in range(ways)]
+    earlier, later = ([x], [x])
+    for _ in range(ways // 2):
+        earlier.append(lax.ppermute(earlier[-1], axis, up))
+    for _ in range((ways - 1) // 2):
+        later.append(lax.ppermute(later[-1], axis, down))
+    line = jnp.concatenate([*earlier[::-1], *later[1:]], axis=dim)
+    return jnp.roll(line, (lax.axis_index(axis) - ways // 2) * x.shape[dim], axis=dim)
 
 
 def orthonormalize(sketched):
@@ -25,7 +38,7 @@
         lax.all_gather(row_right, "col", axis=3, tiled=True),
     )
     col_full_left, col_full_right = (
-        lax.all_gather(col_left, "row", axis=3, tiled=True),
+        ring_gather(col_left, "row", 3),
         lax.all_gather(col_right, "row", axis=3, tiled=True),
     )
     weight_table = (

time: 632 us -> 611 us (0.967)
  waiting for transfers between devices: 190 us -> 155 us
  local copies, waits for them, and re-layouts: 11.6 us -> 19.5 us
    ppermute x0 -> x3, waiting for transfers between devices: none -> 48.5 us  [the longest x2 35.9 us: ring_gather(): earlier.append(lax.ppermute(earlier[-1], axis, up))]
    all_gather x1 -> x0, waiting for transfers between devices: 35.9 us -> none  [on_device(): lax.all_gather(col_left, 'row', axis=3, tiled=True)]
    all_gather x1, waiting for transfers between devices: 35.2 us -> 0.02 us  [on_device(): lax.all_gather(col_right, 'row', axis=3, tiled=True)]
    all_gather x1, waiting for transfers between devices: 48.4 us -> 38.2 us  [on_device(): lax.all_gather(row_right, 'col', axis=3, tiled=True)]
    unnamed x29 -> x40, local copies, waits for them, and re-layouts: 9.61 us -> 16.4 us
  transfers between devices with their start and end apart: 6 -> 8, of which waited for: 6 -> 7; matrix products, arithmetic and copies ran while one was open for 3% -> 4% of each run, Pallas kernels for 0% -> 0%
where the time goes in v1:
time: 611 us; the launch traced here: 605 us
  other arithmetic  355 us (58%)
  waiting for transfers between devices  155 us (25%)
  matrix products  54.6 us (9%)
  local copies, waits for them, and re-layouts  19.5 us (3%)
  between operations  14.4 us (2%)
  starting transfers between devices  6.55 us (1%)
    another operation x7, other arithmetic, orthonormalize(): factor = jnp.linalg.cholesky(gram_mat)  190 us
    another operation x5, other arithmetic, orthonormalize(): sketched = jax.scipy.linalg.solve_triangular(factor, sketched, lower=True)  158 us
    all_gather x1, waiting for transfers between devices, on_device(): lax.all_gather(row_right, 'col', axis=3, tiled=True)  38.2 us
    all_gather x1, waiting for transfers between devices, on_device(): lax.all_gather(row_left, 'col', axis=3, tiled=True)  37.9 us
    ppermute x2, waiting for transfers between devices, ring_gather(): earlier.append(lax.ppermute(earlier[-1], axis, up))  35.9 us
    psum x1, waiting for transfers between devices, on_device(): summed = lax.psum(partial_sketch, 'depth')  23.4 us
    unnamed x40, local copies, waits for them, and re-layouts  16.4 us
    ppermute x1, waiting for transfers between devices, ring_gather(): later.append(lax.ppermute(later[-1], axis, down))  12.6 us
  transfers between devices with their start and end apart: 8, of which 7 were waited for; matrix products, arithmetic and copies ran while one was open for 4% of the time, Pallas kernels for 0%

profile of v1, /device:TPU:0, one launch (start us, length us, event | category | flops | bytes accessed | tf_op | source)
XLA Modules:
  0.0 604.9 jit_solution(13630602385648024625)
XLA Ops:
  7.3 2.0 copy.21
  9.4 1.9 copy.22
  11.3 0.7 all-gather.8.cloned.1.call-update
  12.1 3.0 collective-permute-start
  15.1 17.4 %collective-permute-done = bf16[4,4,64,256]{3,2,1,0:T(8,128)(2,1)S(1)} collective-permute-done((bf16[4,4,64,256]{3,2,1,0:T(8,128)(2,1)S(1)}, bf16[4,4,64,256]{3,2,1,0:T(8,128)(2,1)S(1)}, u32[]{:S(2)}, u32[]{:S(2)}) %collective-permute-start) | collective-permute-done | bytes 524320 | tf_op jit(solution)/shard_map/ppermute | solution.py:18
  32.5 1.9 collective-permute-start.1
  34.4 1.1 collective-permute-start.2
  35.8 18.5 %collective-permute-done.1 = bf16[4,4,64,256]{3,2,1,0:T(8,128)(2,1)} collective-permute-done((bf16[4,4,64,256]{3,2,1,0:T(8,128)(2,1)S(1)}, bf16[4,4,64,256]{3,2,1,0:T(8,128)(2,1)}, u32[]{:S(2)}, u32[]{:S(2)}) %collective-permute-start.1) | collective-permute-done | bytes 524320 | tf_op jit(solution)/shard_map/ppermute | solution.py:18
  54.3 1.1 constant_dynamic-update-slice_fusion.7
  55.6 12.6 %collective-permute-done.2 = bf16[4,4,64,256]{3,2,1,0:T(8,128)(2,1)} collective-permute-done((bf16[4,4,64,256]{3,2,1,0:T(8,128)(2,1)S(1)}, bf16[4,4,64,256]{3,2,1,0:T(8,128)(2,1)}, u32[]{:S(2)}, u32[]{:S(2)}) %collective-permute-start.2) | collective-permute-done | bytes 524320 | tf_op jit(solution)/shard_map/ppermute | solution.py:20
  68.2 1.1 constant_dynamic-update-slice_fusion.4
  69.3 1.1 constant_dynamic-update-slice_fusion.3
  70.6 1.1 constant_dynamic-update-slice_fusion
  71.7 1.9 copy-done.9
  73.7 0.7 fusion.26
  74.4 38.2 %all-gather.6.cloned.1.call-done = bf16[4,4,64,1024]{3,2,0,1:T(8,128)(2,1)} async-done(((bf16[4,4,64,256]{3,2,0,1:T(8,128)(2,1)}), bf16[4,4,64,1024]{3,2,0,1:T(8,128)(2,1)}) %all-gather.6.cloned.1.call-update) | async-done | bytes 2097168 | tf_op jit(solution)/shard_map/all_gather | solution.py:38
  112.6 3.5 bitcast_multiply_fusion
  116.1 1.3 copy-done.6
  117.4 3.3 fusion.15
  120.7 37.9 %all-gather.8.cloned.1.call-done = bf16[4,4,64,1024]{3,2,1,0:T(8,128)(2,1)} async-done(((bf16[4,4,64,256]{3,2,1,0:T(8,128)(2,1)}), bf16[4,4,64,1024]{3,2,1,0:T(8,128)(2,1)}) %all-gather.8.cloned.1.call-update) | async-done | bytes 2097168 | tf_op jit(solution)/shard_map/all_gather | solution.py:37
  158.6 6.2 %bitcast_negate_fusion.1 = f32[4,4,64,1024]{3,2,1,0:T(8,128)} fusion(bf16[4,4,64,1024]{3,2,1,0:T(8,128)(2,1)} %all-gather.8.cloned.1.call-done, f32[4,4,64,4,64]{4,2,1,0,3:T(8,128)} %fusion.15), kind=kOutput, calls=%fused_computation.4 | convolution fusion | flops 3222274048 | bytes 7340032 | tf_op jit(solution)/shard_map/ijkrt,ikrn->ijtn/dot_general | solution.py:55
  164.8 0.3 reduce-scatter.2.cloned.1.call-start
  165.2 2.7 fusion.36
  167.9 23.4 %all-reduce.2.cloned.1.call-done = f32[4,4,64,1024]{3,2,1,0:T(8,128)} async-done(((f32[4,4,64,1024]{3,2,1,0:T(8,128)}), f32[4,4,64,1024]{3,2,1,0:T(8,128)}) %all-reduce.2.cloned.1.call-update) | async-done | bytes 4194320 | tf_op jit(solution)/shard_map/psum | solution.py:65
  191.3 4.1 convolution_add_fusion
  195.4 2.0 copy-done.2
  197.4 4.0 fusion.42
  201.4 0.2 copy.25
  201.6 0.9 fusion.34
  202.5 95.0 %custom-call.8 = f32[4,4,64,64]{3,2,1,0:T(8,128)S(1)} custom-call(f32[4,4,64,64]{3,2,1,0:T(8,128)} %fusion.34), custom_call_target="Cholesky" | custom-call | tf_op jit(solution)/shard_map/jit(cholesky)/cholesky | solution.py:28
  297.8 78.6 %custom-call.9 = f32[4,4,1,64,64]{3,4,2,1,0:T(8,128)S(1)} custom-call(f32[4,4,1,64,64]{4,3,2,1,0:T(8,128)S(1)} %select_bitcast_fusion.1), custom_call_target="InvertDiagBlocksLowerTriangular" | custom-call | tf_op jit(solution)/shard_map/jit(_solve_triangular)/vmap(vmap())/triangular_solve | solution.py:29
  376.5 5.5 fusion.32
  382.0 2.0 copy-done.1
  384.0 4.0 fusion.43
  388.2 0.9 fusion.31
  389.1 94.5 %custom-call.10 = f32[4,4,64,64]{3,2,1,0:T(8,128)S(1)} custom-call(f32[4,4,64,64]{3,2,1,0:T(8,128)} %fusion.31), custom_call_target="Cholesky" | custom-call | tf_op jit(solution)/shard_map/jit(cholesky)/cholesky | solution.py:28
  483.9 78.6 %custom-call.11 = f32[4,4,1,64,64]{3,4,2,1,0:T(8,128)S(1)} custom-call(f32[4,4,1,64,64]{4,3,2,1,0:T(8,128)S(1)} %select_bitcast_fusion), custom_call_target="InvertDiagBlocksLowerTriangular" | custom-call | tf_op jit(solution)/shard_map/jit(_solve_triangular)/vmap(vmap())/triangular_solve | solution.py:29
  562.6 5.8 fusion.29
  568.4 3.5 fusion
  571.9 1.4 copy.59
  573.5 3.5 fusion.12
  577.0 3.7 fusion.2
  580.7 3.4 dynamic-slice_multiply_fusion
  584.1 1.8 fusion.17
  585.9 2.3 fusion.10
  588.2 5.8 reduce-scatter.2.cloned.1.call-done
  594.1 2.6 add_multiply_fusion
  596.7 1.5 copy.30
  (53 shorter events, 2.0 us)
Async XLA Ops:
  7.2 184.1 %copy-start = (bf16[4,4,64,1024]{3,2,1,0:T(8,128)(2,1)S(1)}, bf16[4,4,64,1024]{3,2,1,0:T(8,128)(2,1)}, u32[]{:S(2)}) copy-start(bf16[4,4,64,1024]{3,2,1,0:T(8,128)(2,1)} %param.12) | copy-start | bytes 6291460
  7.2 4.9 copy-start.11
  7.2 28.3 %copy-start.13 = (s32[4,4]{1,0:T(4,128)S(1)}, s32[4,4]{1,0:T(4,128)}, u32[]{:S(2)}) copy-start(s32[4,4]{1,0:T(4,128)} %param.18) | copy-start | bytes 196
  7.2 28.4 %copy-start.14 = (s32[4,4]{1,0:T(4,128)S(1)}, s32[4,4]{1,0:T(4,128)}, u32[]{:S(2)}) copy-start(s32[4,4]{1,0:T(4,128)} %param.19) | copy-start | bytes 196
  7.2 67.2 %all-gather.4.cloned.1.call-start = ((), (), s32[]{:S(2)}) async-start(), calls=%async_computation.1 | async-start | bytes 2621440 | tf_op jit(solution)/shard_map/all_gather | solution.py:42
  9.3 103.3 %all-gather.6.cloned.1.call-start = ((), (), s32[]{:S(2)}) async-start(), calls=%async_computation.2 | async-start | bytes 2621440 | tf_op jit(solution)/shard_map/all_gather | solution.py:38
  11.3 147.4 %all-gather.8.cloned.1.call-start = ((), (), s32[]{:S(2)}) async-start(), calls=%async_computation.3 | async-start | bytes 2621440 | tf_op jit(solution)/shard_map/all_gather | solution.py:37
  12.0 179.3 %all-reduce.2.cloned.1.call-start = ((), (), s32[]{:S(2)}) async-start(), calls=%async_computation.4 | async-start | bytes 8388608 | tf_op jit(solution)/shard_map/psum | solution.py:65
  12.1 20.4 %collective-permute-start = (bf16[4,4,64,256]{3,2,1,0:T(8,128)(2,1)S(1)}, bf16[4,4,64,256]{3,2,1,0:T(8,128)(2,1)S(1)}, u32[]{:S(2)}, u32[]{:S(2)}) collective-permute-start(bf16[4,4,64,256]{3,2,1,0:T(8,128)(2,1)S(1)} %copy-done.11), channel_id=1, source_target_pairs={{0,4},{4,8},{8,12},{12,0},{1,5},{5,9},{9,13},{13,1},{2,6},{6,10},{... | collective-permute-start | bytes 1572872 | tf_op jit(solution)/shard_map/ppermute | solution.py:18
  32.5 21.9 %collective-permute-start.1 = (bf16[4,4,64,256]{3,2,1,0:T(8,128)(2,1)S(1)}, bf16[4,4,64,256]{3,2,1,0:T(8,128)(2,1)}, u32[]{:S(2)}, u32[]{:S(2)}) collective-permute-start(bf16[4,4,64,256]{3,2,1,0:T(8,128)(2,1)S(1)} %collective-permute-done), channel_id=1, source_target_pairs={{0,4},{4,8},{8,12},{12,0},{1,5},{5,9},{9,13},{13,1},{2,6},{6,10},{... | collective-permute-start | bytes 1572872 | tf_op jit(solution)/shard_map/ppermute | solution.py:18
  34.4 33.8 %collective-permute-start.2 = (bf16[4,4,64,256]{3,2,1,0:T(8,128)(2,1)S(1)}, bf16[4,4,64,256]{3,2,1,0:T(8,128)(2,1)}, u32[]{:S(2)}, u32[]{:S(2)}) collective-permute-start(bf16[4,4,64,256]{3,2,1,0:T(8,128)(2,1)S(1)} %copy-done.11), channel_id=1, source_target_pairs={{0,12},{4,0},{8,4},{12,8},{1,13},{5,1},{9,5},{13,9},{2,14},{6,2},{... | collective-permute-start | bytes 1572872 | tf_op jit(solution)/shard_map/ppermute | solution.py:20
  69.3 4.4 copy-start.12
  71.7 2.0 copy-start.9
  116.1 1.3 copy-start.6
  164.8 429.2 %reduce-scatter.2.cloned.1.call-start = ((), (), s32[]{:S(2)}) async-start(), calls=%async_computation.5 | async-start | bytes 6291456 | tf_op jit(solution)/shard_map/reduce_scatter | solution.py:92
  195.4 2.0 copy-start.2
  382.0 2.0 copy-start.1
  562.6 5.8 copy-start.5
  568.4 3.5 copy-start.3
  571.9 1.6 copy-start.7
  573.5 3.5 copy-start.10
  580.7 3.4 copy-start.4
  584.1 1.8 copy-start.8
Sparse Core Ops, SparseCore 0:
  10.4 53.7 all-gather.3
  66.3 46.2 all-gather.5
  114.2 44.4 all-gather.7
  164.9 26.2 all-reduce.1
  580.8 13.2 reduce-scatter.1
